TPU v7x, 256 devices: a whole 4x4x8 slice. The times are simulated.
256 devices in a mesh: row: 8 (over z), col: 32 (over x, y, core).
Axes of the slice: x: 4, y: 4, z: 8, core: 2. Of those that a mesh axis runs over, the one named last changes fastest.
Arguments:
- latitude: bfloat16 [16384, 256], P(('row', 'col')), may hold values from -4 to 4
- longitude: bfloat16 [16384, 512], P(('row', 'col')), may hold values from -4 to 4
- weight: bfloat16 [16384], P(('row', 'col')), may hold values from 0.29882812 to 3
- harmonic_index: int32 [2, 24576], P(None, 'col'), may hold values from 0 to 511, as said below
Outputs:
- coefficients: float32 [512, 24576], P(None, 'col')
- residual: float32 [16384, 24576], P('row', 'col')
Inputs may be any that keep to these rules, and one draw needn't show every extreme that they name: The pairs (harmonic_index[0, j], harmonic_index[1, j]) are distinct over all 24576 columns; row 0 is below 256, and harmonic_index[1, j] // 2 never exceeds harmonic_index[0, j].
All inputs are finite; a program needn't handle non-finite values.
Results may differ from a plain program's by a relative error of at most 0.0003.
Values may be sent and summed in bfloat16 or wider, within the bound.
No kernel may reach another device: no remote copies, remote signals or barrier semaphores. Data moves between devices by JAX's collectives and lax.ppermute only.
A program may use at most 128 MiB of HBM per device.

v0:
```python
import math
import jax
import jax.numpy as jnp
from jax import lax
from jax.sharding import PartitionSpec as P

PANEL = 256


def in_one_piece(arrays, axis, dim, along):
    widths = [math.prod(a.shape[along:]) for a in arrays]
    both = jnp.concatenate(
        [a.reshape(*a.shape[:along], w) for a, w in zip(arrays, widths)], axis=along
    )
    result = lax.all_gather(both, axis, axis=dim, tiled=True)
    tiles = jnp.split(result, [sum(widths[:k]) for k in range(1, len(widths))], axis=along)
    return tuple(
        (b.reshape(*result.shape[:along], *a.shape[along:]) for a, b in zip(arrays, tiles))
    )


def picked(array, axis, root):
    return lax.dynamic_index_in_dim(lax.all_gather(array, axis), root, 0, keepdims=False)


def synthesize(latitude, longitude, weight, column_index):
    degree_hot = (
        column_index[0][None, :] == jnp.arange(latitude.shape[1], dtype=jnp.int32)[:, None]
    ).astype(jnp.bfloat16)
    order_hot = (
        column_index[1][None, :] == jnp.arange(longitude.shape[1], dtype=jnp.int32)[:, None]
    ).astype(jnp.bfloat16)
    picked_degree = jnp.dot(latitude, degree_hot, preferred_element_type=jnp.float32)
    picked_order = jnp.dot(longitude, order_hot, preferred_element_type=jnp.float32)
    return weight.astype(jnp.float32)[:, None] * picked_degree * picked_order


def orthonormal(panel_cols, gram_sum):
    lower_factor = jnp.linalg.cholesky(gram_sum)
    return lax.linalg.triangular_solve(lower_factor, panel_cols.T, left_side=True, lower=True)


def remove_span(design, basis_t, top_rows):
    return design - jnp.dot(
        basis_t.T, top_rows, precision=lax.Precision.HIGHEST, preferred_element_type=jnp.float32
    )


def shards(latitude, longitude, weight, harmonic_index):
    tables = in_one_piece((latitude, longitude, weight), "col", 0, 1)
    lead_index = picked(harmonic_index[:, : 2 * PANEL], "col", 0)
    lead_cols = synthesize(tables[0], tables[1], tables[2], lead_index)
    design = synthesize(tables[0], tables[1], tables[2], harmonic_index)
    local_gram = jnp.dot(
        lead_cols.T, lead_cols, precision=lax.Precision.HIGHEST, preferred_element_type=jnp.float32
    )
    gram_sum = lax.psum(local_gram, "row")
    basis_t = orthonormal(lead_cols, gram_sum)
    local_rows = jnp.dot(
        basis_t, design, precision=lax.Precision.HIGHEST, preferred_element_type=jnp.float32
    )
    coefficients = lax.psum(local_rows, "row")
    residual = remove_span(design, basis_t, coefficients)
    return (coefficients, residual)


def solution(mesh):
    return jax.shard_map(
        shards,
        mesh=mesh,
        in_specs=(
            P(("row", "col"), None),
            P(("row", "col"), None),
            P(("row", "col")),
            P(None, "col"),
        ),
        out_specs=(P(None, "col"), P("row", "col")),
        check_vma=False,
    )
```

profile of v0, /device:TPU:2, one launch (start us, length us, event | category | flops | bytes accessed | tf_op | source)
XLA Modules:
  0.0 433.0 jit_solution(3629395771598168058)
XLA Ops:
  8.0 1.5 pad_maximum_fusion.3
  10.2 24.6 %all-gather.1 = s32[32,2,512]{2,1,0:T(2,128)S(1)} all-gather(s32[1,2,512]{2,1,0:T(2,128)S(1)} %slice_bitcast_fusion.8), channel_id=2, replica_groups=mesh['row'=8,'col'=32] {'col'}, dimensions={0}, use_global_device_ids=true | all-gather | bytes 135168 | tf_op jit(solution)/shard_map/all_gather | solution.py:23
  35.6 28.7 %all-gather.4.cloned.1.call-done = bf16[2048,769]{1,0:T(8,128)(2,1)} async-done(((bf16[64,769]{1,0:T(8,128)(2,1)}), bf16[2048,769]{1,0:T(8,128)(2,1)}) %all-gather.4.cloned.1.call-update) | async-done | bytes 3149840 | tf_op jit(solution)/shard_map/all_gather | solution.py:15
  64.3 1.4 convert_reduce_fusion
  65.7 2.0 fusion.20
  69.0 1.9 copy-done
  70.9 8.0 %fusion.49 = f32[512,512]{0,1:T(8,128)} fusion(f32[2048,512]{1,0:T(8,128)S(1)} %multiply_multiply_fusion.1), kind=kOutput, calls=%fused_computation.94 | convolution fusion | flops 6442450944 | bytes 5242880 | tf_op jit(solution)/shard_map/dot_general | solution.py:54
  79.3 2.4 fusion.18
  81.7 4.7 %multiply_multiply_fusion = f32[2048,768]{1,0:T(8,128)} fusion(f32[2048,768]{1,0:T(8,128)S(1)} %fusion.18, f32[2048]{0:T(1024)S(1)} %convert_reduce_fusion, bf16[2048,769]{1,0:T(8,128)(2,1)S(1)} %copy-done.3, s32[768]{0:T(1024)S(1)} %get-tuple-element.10), kind=kOutput, calls=%fused_computation.2 | convolution fusion | flops 1614151680 | bytes 14692352 | tf_op jit(solution)/shard_map/dot_general | solution.py:34
  86.4 68.5 %all-reduce.4.cloned.1.call-done = f32[512,512]{0,1:T(8,128)} async-done(((f32[512,512]{0,1:T(8,128)}), f32[512,512]{0,1:T(8,128)}) %all-reduce.4.cloned.1.call-update) | async-done | bytes 1048592 | tf_op jit(solution)/shard_map/psum | solution.py:57
  154.9 1.6 copy.14
  156.4 1.4 fusion.17
  157.9 11.7 %cholesky.104 = f32[128,128]{1,0:T(8,128)S(1)} custom-call(f32[128,128]{1,0:T(8,128)S(1)} %cholesky.266), custom_call_target="Cholesky" | custom-call | tf_op jit(solution)/shard_map/jit(cholesky)/cholesky | solution.py:39
  169.6 9.8 %custom-call.30 = f32[1,128,128]{1,2,0:T(8,128)S(1)} custom-call(f32[1,128,128]{2,1,0:T(8,128)S(1)} %get-tuple-element.33), custom_call_target="InvertDiagBlocksLowerTriangular" | custom-call | tf_op jit(solution)/shard_map/jit(cholesky)/cholesky | solution.py:39
  180.3 12.2 %cholesky.217 = f32[128,128]{1,0:T(8,128)S(1)} custom-call(f32[128,128]{1,0:T(8,128)S(1)} %cholesky.270), custom_call_target="Cholesky" | custom-call | tf_op jit(solution)/shard_map/jit(cholesky)/cholesky | solution.py:39
  192.4 9.8 %custom-call.31 = f32[1,128,128]{1,2,0:T(8,128)S(1)} custom-call(f32[1,128,128]{2,1,0:T(8,128)S(1)} %get-tuple-element.30), custom_call_target="InvertDiagBlocksLowerTriangular" | custom-call | tf_op jit(solution)/shard_map/jit(cholesky)/cholesky | solution.py:39
  202.9 11.7 %cholesky.238 = f32[128,128]{1,0:T(8,128)S(1)} custom-call(f32[128,128]{1,0:T(8,128)S(1)} %cholesky.275), custom_call_target="Cholesky" | custom-call | tf_op jit(solution)/shard_map/jit(cholesky)/cholesky | solution.py:39
  215.3 9.8 %custom-call.32 = f32[1,128,128]{1,2,0:T(8,128)S(1)} custom-call(f32[1,128,128]{2,1,0:T(8,128)S(1)} %get-tuple-element.27), custom_call_target="InvertDiagBlocksLowerTriangular" | custom-call | tf_op jit(solution)/shard_map/jit(cholesky)/cholesky | solution.py:39
  225.7 11.9 %cholesky.255 = f32[128,128]{1,0:T(8,128)S(1)} custom-call(f32[128,128]{1,0:T(8,128)S(1)} %convolution_subtract_fusion.5), custom_call_target="Cholesky" | custom-call | tf_op jit(solution)/shard_map/jit(cholesky)/cholesky | solution.py:39
  241.7 10.3 %while.1 = (s32[]{:T(128)}, f32[512,512]{1,0:T(8,128)S(1)}, s32[4,2]{0,1:T(2,128)S(1)}, f32[4,128,128]{2,1,0:T(8,128)}, s32[]{:T(128)}) while((s32[]{:T(128)}, f32[512,512]{1,0:T(8,128)S(1)}, s32[4,2]{0,1:T(2,128)S(1)}, f32[4,128,128]{2,1,0:T(8,128)}, s32[]{:T(128)}) %tuple.33), condition=%wide.while_cond, body=%wide.while_body.sunk | while | flops 2 | bytes 132205 | solution.py:40
  242.3 2.0 bitcast_dynamic-update-slice_fusion.2
  244.9 2.0 bitcast_dynamic-update-slice_fusion.2
  247.5 2.0 bitcast_dynamic-update-slice_fusion.2
  250.1 2.0 bitcast_dynamic-update-slice_fusion.2
  252.0 40.2 %custom-call.33 = f32[4,128,128]{1,2,0:T(8,128)S(1)} custom-call(f32[4,128,128]{2,1,0:T(8,128)} %get-tuple-element.9), custom_call_target="InvertDiagBlocksLowerTriangular" | custom-call | tf_op jit(solution)/shard_map/triangular_solve | solution.py:40
  292.2 2.4 fusion.15
  294.7 3.0 convolution_subtract_fusion.2
  298.8 3.5 convolution_subtract_fusion.1
  303.5 6.6 %fusion.6 = f32[128,2048]{0,1:T(8,128)S(1)} fusion(f32[128,2048]{1,0:T(8,128)S(1)} %fusion.35, f32[128,2048]{1,0:T(8,128)S(1)} %fusion.37, f32[128,2048]{1,0:T(8,128)S(1)} %fusion.15, f32[512,2048]{0,1:T(8,128)S(1)} %bitcast.61, f32[512,512]{1,0:T(8,128)} %copy-done.6), kind=kOutput, calls=%fused_computation.12 | convolution fusion | flops 1209794560 | bytes 5439488 | tf_op jit(solution)/shard_map/triangular_solve | solution.py:40
  312.2 11.6 %fusion.9 = f32[512,768]{1,0:T(8,128)} fusion(f32[2048,768]{1,0:T(8,128)S(1)} %bitcast.63, f32[128,2048]{1,0:T(8,128)S(1)} %fusion.34, f32[128,2048]{1,0:T(8,128)S(1)} %fusion.35, f32[128,2048]{1,0:T(8,128)S(1)} %fusion.37, f32[128,2048]{1,0:T(8,128)S(1)} %fusion.15), kind=kOutput, calls=%fused_computation.15 | convolution fusion | flops 9666822144 | bytes 12058624 | tf_op jit(solution)/shard_map/dot_general | solution.py:59
  323.8 77.3 %all-reduce.6.cloned.1.call-done = f32[512,768]{1,0:T(8,128)} async-done(((f32[512,768]{1,0:T(8,128)}), f32[512,768]{1,0:T(8,128)}) %all-reduce.6.cloned.1.call-update) | async-done | bytes 1572880 | tf_op jit(solution)/shard_map/psum | solution.py:62
  401.0 23.9 %convolution_subtract_fusion = f32[2048,768]{1,0:T(8,128)} fusion(f32[2048,768]{1,0:T(8,128)} %multiply_multiply_fusion, f32[512,768]{1,0:T(8,128)} %all-reduce.6.cloned.1.call-done, f32[128,2048]{1,0:T(8,128)} %copy-done.5, f32[128,2048]{1,0:T(8,128)S(1)} %fusion.35, f32[128,2048]{1,0:T(8,128)S(1)} %fusion.37, f32[128,2048]{1,0:T(8,128)S(1)} %fusion.15), kind=kOutput, calls=%fused_computation.5 | convolution fusion | flops 9668395008 | bytes 18350080 | tf_op jit(solution)/shard_map/dot_general | solution.py:44
  (62 shorter events, 16.0 us)
Async XLA Ops:
  7.2 57.1 %all-gather.4.cloned.1.call-start = ((), (), s32[]{:S(2)}) async-start(), calls=%async_computation | async-start | bytes 3784704 | tf_op jit(solution)/shard_map/all_gather | solution.py:15
  9.5 145.4 %all-reduce.4.cloned.1.call-start = ((), (), s32[]{:S(2)}) async-start(), calls=%async_computation.1 | async-start | bytes 2097152 | tf_op jit(solution)/shard_map/psum | solution.py:57
  64.3 3.4 copy-start.2
  69.0 1.9 copy-start
  79.0 322.0 %all-reduce.6.cloned.1.call-start = ((), (), s32[]{:S(2)}) async-start(), calls=%async_computation.2 | async-start | bytes 3145728 | tf_op jit(solution)/shard_map/psum | solution.py:62
  79.3 2.4 copy-start.3
  252.0 46.8 %copy-start.6 = (f32[512,512]{1,0:T(8,128)}, f32[512,512]{1,0:T(8,128)S(1)}, u32[]{:S(2)}) copy-start(f32[512,512]{1,0:T(8,128)S(1)} %get-tuple-element.92) | copy-start | bytes 3145732
  292.2 6.6 %copy-start.1 = (f32[2048,512]{1,0:T(8,128)S(1)}, f32[2048,512]{1,0:T(8,128)}, u32[]{:S(2)}) copy-start(f32[2048,512]{1,0:T(8,128)} %copy-done) | copy-start | bytes 12582916
  298.8 13.4 %slice-start = ((s8[6291456]{0:T(1024)(128)(4,1)}), s8[4194304]{0:T(1024)(128)(4,1)S(1)}, s32[]{:S(2)}) async-start(s8[6291456]{0:T(1024)(128)(4,1)} %bitcast.62), calls=%async_computation.3 | async-start | bytes 8388608
  303.4 8.7 %slice-start.1 = ((s8[6291456]{0:T(1024)(128)(4,1)}), s8[2097152]{0:T(1024)(128)(4,1)S(1)}, s32[]{:S(2)}) async-start(s8[6291456]{0:T(1024)(128)(4,1)} %bitcast.62), calls=%async_computation.4 | async-start | bytes 4194304
  311.2 1.0 copy-start.5
  401.0 23.9 %copy-start.4 = (f32[512,768]{1,0:T(8,128)S(1)}, f32[512,768]{1,0:T(8,128)}, u32[]{:S(2)}) copy-start(f32[512,768]{1,0:T(8,128)} %all-reduce.6.cloned.1.call-done) | copy-start | bytes 4718596
Sparse Core Ops, SparseCore 0:
  11.1 53.1 all-gather.3
  79.1 75.7 all-reduce.3
  323.9 77.1 all-reduce.5
where the time goes:
time: 441 us; the launch traced here: 433 us
  waiting for transfers between devices  174 us (39%)
  other arithmetic  124 us (28%)
  matrix products  74.6 us (17%)
  blocking collectives  24.6 us (6%)
  local copies, waits for them, and re-layouts  18.3 us (4%)
  between operations  17.1 us (4%)
    another operation x14, other arithmetic, orthonormal(): lower_factor = jnp.linalg.cholesky(gram_sum)  79 us
    psum x1, waiting for transfers between devices, shards(): coefficients = lax.psum(local_rows, 'row')  77.3 us
    psum x1, waiting for transfers between devices, shards(): gram_sum = lax.psum(local_gram, 'row')  68.5 us
    another operation x3, other arithmetic, orthonormal(): lax.linalg.triangular_solve(lower_factor, panel_cols.T, left_side=True, l...  40.3 us
    all_gather x1, waiting for transfers between devices, in_one_piece(): result = lax.all_gather(both, axis, axis=dim, tiled=True)  28.7 us
    all_gather x1, blocking collectives, picked(): lax.all_gather(array, axis)  24.6 us
    dot_general x1, matrix products, remove_span(): jnp.dot(basis_t.T, top_rows, precision=lax.Precision.HIGHEST, preferred_e...  23.9 us
    another operation x7, matrix products, orthonormal(): lax.linalg.triangular_solve(lower_factor, panel_cols.T, left_side=True, l...  18.9 us
  transfers between devices with their start and end apart: 3, of which 3 were waited for; matrix products, arithmetic and copies ran while one was open for 2% of the time, Pallas kernels for 0%

commit v1 on v0

--- a/solution.py
+++ b/solution.py
@@ -54,7 +54,9 @@
     local_gram = jnp.dot(
         lead_cols.T, lead_cols, precision=lax.Precision.HIGHEST, preferred_element_type=jnp.float32
     )
-    gram_sum = lax.psum(local_gram, "row")
+    gram_sum = local_gram
+    for hop in (1, 2, 4):
+        gram_sum = gram_sum + lax.ppermute(gram_sum, "row", [(dev, dev ^ hop) for dev in range(8)])
     basis_t = orthonormal(lead_cols, gram_sum)
     local_rows = jnp.dot(
         basis_t, design, precision=lax.Precision.HIGHEST, preferred_element_type=jnp.float32

time: 441 us -> 486 us (1.10)
  waiting for transfers between devices: 174 us -> 213 us
  starting transfers between devices: 0.34 us -> 10.3 us
    ppermute x0 -> x3, waiting for transfers between devices: none -> 108 us  [shards(): lax.ppermute(gram_sum, 'row', [(dev, dev ^ hop) for dev in range(8)])]
    psum x1 -> x0, waiting for transfers between devices: 68.5 us -> none  [shards(): gram_sum = lax.psum(local_gram, 'row')]
    ppermute x0 -> x3, starting transfers between devices: none -> 10.3 us  [shards(): lax.ppermute(gram_sum, 'row', [(dev, dev ^ hop) for dev in range(8)])]
  transfers between devices with their start and end apart: 3 -> 5, of which waited for: 3 -> 5; matrix products, arithmetic and copies ran while one was open for 2% -> 2% of each run, Pallas kernels for 0% -> 0%
where the time goes in v1:
time: 486 us; the launch traced here: 477 us
  waiting for transfers between devices  213 us (44%)
  other arithmetic  123 us (25%)
  matrix products  73.6 us (15%)
  blocking collectives  24.6 us (5%)
  between operations  17.3 us (4%)
  local copies, waits for them, and re-layouts  14.3 us (3%)
  starting transfers between devices  10.3 us (2%)
    ppermute x3, waiting for transfers between devices, shards(): lax.ppermute(gram_sum, 'row', [(dev, dev ^ hop) for dev in range(8)])  108 us
    another operation x14, other arithmetic, orthonormal(): lower_factor = jnp.linalg.cholesky(gram_sum)  79 us
    psum x1, waiting for transfers between devices, shards(): coefficients = lax.psum(local_rows, 'row')  75.8 us
    another operation x3, other arithmetic, orthonormal(): lax.linalg.triangular_solve(lower_factor, panel_cols.T, left_side=True, l...  40.3 us
    all_gather x1, waiting for transfers between devices, in_one_piece(): result = lax.all_gather(both, axis, axis=dim, tiled=True)  29.5 us
    all_gather x1, blocking collectives, picked(): lax.all_gather(array, axis)  24.6 us
    dot_general x1, matrix products, remove_span(): jnp.dot(basis_t.T, top_rows, precision=lax.Precision.HIGHEST, preferred_e...  23.9 us
    another operation x7, matrix products, orthonormal(): lax.linalg.triangular_solve(lower_factor, panel_cols.T, left_side=True, l...  18.9 us
  transfers between devices with their start and end apart: 5, of which 5 were waited for; matrix products, arithmetic and copies ran while one was open for 2% of the time, Pallas kernels for 0%

profile of v1, /device:TPU:2, one launch (start us, length us, event | category | flops | bytes accessed | tf_op | source)
XLA Modules:
  0.0 476.6 jit_solution(11968567038433805005)
XLA Ops:
  10.2 24.6 %all-gather.1 = s32[32,2,512]{2,1,0:T(2,128)S(1)} all-gather(s32[1,2,512]{2,1,0:T(2,128)S(1)} %slice_bitcast_fusion.8), channel_id=2, replica_groups=mesh['row'=8,'col'=32] {'col'}, dimensions={0}, use_global_device_ids=true | all-gather | bytes 135168 | tf_op jit(solution)/shard_map/all_gather | solution.py:23
  34.8 29.5 %all-gather.4.cloned.1.call-done = bf16[2048,769]{1,0:T(8,128)(2,1)} async-done(((bf16[64,769]{1,0:T(8,128)(2,1)}), bf16[2048,769]{1,0:T(8,128)(2,1)}) %all-gather.4.cloned.1.call-update) | async-done | bytes 3149840 | tf_op jit(solution)/shard_map/all_gather | solution.py:15
  65.7 2.0 fusion.20
  69.0 7.1 %fusion.54 = f32[512,512]{0,1:T(8,128)S(1)} fusion(f32[2048,512]{1,0:T(8,128)S(1)} %multiply_multiply_fusion.1), kind=kOutput, calls=%fused_computation.97 | convolution fusion | flops 6442450944 | bytes 5242880 | tf_op jit(solution)/shard_map/dot_general | solution.py:54
  76.1 1.6 collective-permute-start
  77.8 23.8 %collective-permute-done = f32[512,512]{0,1:T(8,128)S(1)} collective-permute-done((f32[512,512]{0,1:T(8,128)S(1)}, f32[512,512]{0,1:T(8,128)S(1)}, u32[]{:S(2)}, u32[]{:S(2)}) %collective-permute-start) | collective-permute-done | bytes 1048608 | tf_op jit(solution)/shard_map/ppermute | solution.py:59
  101.7 2.6 collective-permute-start.1
  104.4 45.3 %collective-permute-done.1 = f32[512,512]{0,1:T(8,128)S(1)} collective-permute-done((f32[512,512]{0,1:T(8,128)S(1)}, f32[512,512]{0,1:T(8,128)S(1)}, u32[]{:S(2)}, u32[]{:S(2)}) %collective-permute-start.1) | collective-permute-done | bytes 1048608 | tf_op jit(solution)/shard_map/ppermute | solution.py:59
  149.9 6.0 %collective-permute-start.2 = (f32[512,512]{0,1:T(8,128)S(1)}, f32[512,512]{0,1:T(8,128)S(1)}, u32[]{:S(2)}, u32[]{:S(2)}) collective-permute-start(f32[512,512]{0,1:T(8,128)S(1)} %add.54), channel_id=1, source_target_pairs={{0,128},{32,160},{64,192},{96,224},{128,0},{160,32},{192,64},{224,... | collective-permute-start | bytes 3145736 | tf_op jit(solution)/shard_map/ppermute | solution.py:59
  155.9 2.4 fusion.18
  158.3 4.7 multiply_multiply_fusion
  163.0 39.0 %collective-permute-done.2 = f32[512,512]{0,1:T(8,128)S(1)} collective-permute-done((f32[512,512]{0,1:T(8,128)S(1)}, f32[512,512]{0,1:T(8,128)S(1)}, u32[]{:S(2)}, u32[]{:S(2)}) %collective-permute-start.2) | collective-permute-done | bytes 1048608 | tf_op jit(solution)/shard_map/ppermute | solution.py:59
  202.9 11.7 %cholesky.104 = f32[128,128]{1,0:T(8,128)S(1)} custom-call(f32[128,128]{1,0:T(8,128)S(1)} %cholesky.266), custom_call_target="Cholesky" | custom-call | tf_op jit(solution)/shard_map/jit(cholesky)/cholesky | solution.py:39
  214.6 9.8 %custom-call.30 = f32[1,128,128]{1,2,0:T(8,128)S(1)} custom-call(f32[1,128,128]{2,1,0:T(8,128)S(1)} %get-tuple-element.33), custom_call_target="InvertDiagBlocksLowerTriangular" | custom-call | tf_op jit(solution)/shard_map/jit(cholesky)/cholesky | solution.py:39
  225.2 12.1 %cholesky.217 = f32[128,128]{1,0:T(8,128)S(1)} custom-call(f32[128,128]{1,0:T(8,128)S(1)} %cholesky.270), custom_call_target="Cholesky" | custom-call | tf_op jit(solution)/shard_map/jit(cholesky)/cholesky | solution.py:39
  237.3 9.8 %custom-call.31 = f32[1,128,128]{1,2,0:T(8,128)S(1)} custom-call(f32[1,128,128]{2,1,0:T(8,128)S(1)} %get-tuple-element.30), custom_call_target="InvertDiagBlocksLowerTriangular" | custom-call | tf_op jit(solution)/shard_map/jit(cholesky)/cholesky | solution.py:39
  247.8 11.7 %cholesky.238 = f32[128,128]{1,0:T(8,128)S(1)} custom-call(f32[128,128]{1,0:T(8,128)S(1)} %cholesky.275), custom_call_target="Cholesky" | custom-call | tf_op jit(solution)/shard_map/jit(cholesky)/cholesky | solution.py:39
  260.2 9.8 %custom-call.32 = f32[1,128,128]{1,2,0:T(8,128)S(1)} custom-call(f32[1,128,128]{2,1,0:T(8,128)S(1)} %get-tuple-element.27), custom_call_target="InvertDiagBlocksLowerTriangular" | custom-call | tf_op jit(solution)/shard_map/jit(cholesky)/cholesky | solution.py:39
  270.6 11.9 %cholesky.255 = f32[128,128]{1,0:T(8,128)S(1)} custom-call(f32[128,128]{1,0:T(8,128)S(1)} %slice_subtract_fusion.2), custom_call_target="Cholesky" | custom-call | tf_op jit(solution)/shard_map/jit(cholesky)/cholesky | solution.py:39
  286.6 10.2 %while.1 = (s32[]{:T(128)}, f32[512,512]{1,0:T(8,128)S(1)}, s32[4,2]{0,1:T(2,128)S(1)}, f32[4,128,128]{2,1,0:T(8,128)}, s32[]{:T(128)}) while((s32[]{:T(128)}, f32[512,512]{1,0:T(8,128)S(1)}, s32[4,2]{0,1:T(2,128)S(1)}, f32[4,128,128]{2,1,0:T(8,128)}, s32[]{:T(128)}) %tuple.33), condition=%wide.while_cond, body=%wide.while_body.sunk | while | flops 2 | bytes 132205 | solution.py:40
  287.2 1.9 bitcast_dynamic-update-slice_fusion.2
  289.7 1.9 bitcast_dynamic-update-slice_fusion.2
  292.3 1.9 bitcast_dynamic-update-slice_fusion.2
  294.9 1.9 bitcast_dynamic-update-slice_fusion.2
  296.8 40.2 %custom-call.33 = f32[4,128,128]{1,2,0:T(8,128)S(1)} custom-call(f32[4,128,128]{2,1,0:T(8,128)} %get-tuple-element.9), custom_call_target="InvertDiagBlocksLowerTriangular" | custom-call | tf_op jit(solution)/shard_map/triangular_solve | solution.py:40
  337.0 2.4 fusion.15
  339.4 3.0 convolution_subtract_fusion.2
  343.6 3.5 convolution_subtract_fusion.1
  348.2 6.6 %fusion.6 = f32[128,2048]{0,1:T(8,128)S(1)} fusion(f32[128,2048]{1,0:T(8,128)S(1)} %fusion.37, f32[128,2048]{1,0:T(8,128)S(1)} %fusion.39, f32[128,2048]{1,0:T(8,128)S(1)} %fusion.15, f32[512,2048]{0,1:T(8,128)S(1)} %bitcast.61, f32[512,512]{1,0:T(8,128)} %copy-done.6), kind=kOutput, calls=%fused_computation.12 | convolution fusion | flops 1209794560 | bytes 5439488 | tf_op jit(solution)/shard_map/triangular_solve | solution.py:40
  356.9 11.6 %fusion.9 = f32[512,768]{1,0:T(8,128)} fusion(f32[2048,768]{1,0:T(8,128)S(1)} %bitcast.63, f32[128,2048]{1,0:T(8,128)S(1)} %fusion.36, f32[128,2048]{1,0:T(8,128)S(1)} %fusion.37, f32[128,2048]{1,0:T(8,128)S(1)} %fusion.39, f32[128,2048]{1,0:T(8,128)S(1)} %fusion.15), kind=kOutput, calls=%fused_computation.15 | convolution fusion | flops 9666822144 | bytes 12058624 | tf_op jit(solution)/shard_map/dot_general | solution.py:61
  368.5 75.8 %all-reduce.3.cloned.1.call-done = f32[512,768]{1,0:T(8,128)} async-done(((f32[512,768]{1,0:T(8,128)}), f32[512,768]{1,0:T(8,128)}) %all-reduce.3.cloned.1.call-update) | async-done | bytes 1572880 | tf_op jit(solution)/shard_map/psum | solution.py:64
  444.3 23.9 %convolution_subtract_fusion = f32[2048,768]{1,0:T(8,128)} fusion(f32[2048,768]{1,0:T(8,128)} %multiply_multiply_fusion, f32[512,768]{1,0:T(8,128)} %all-reduce.3.cloned.1.call-done, f32[128,2048]{1,0:T(8,128)} %copy-done.5, f32[128,2048]{1,0:T(8,128)S(1)} %fusion.37, f32[128,2048]{1,0:T(8,128)S(1)} %fusion.39, f32[128,2048]{1,0:T(8,128)S(1)} %fusion.15), kind=kOutput, calls=%fused_computation.5 | convolution fusion | flops 9668395008 | bytes 18350080 | tf_op jit(solution)/shard_map/dot_general | solution.py:44
  (70 shorter events, 19.1 us)
Async XLA Ops:
  7.2 57.1 %all-gather.4.cloned.1.call-start = ((), (), s32[]{:S(2)}) async-start(), calls=%async_computation | async-start | bytes 3784704 | tf_op jit(solution)/shard_map/all_gather | solution.py:15
  9.5 434.8 %all-reduce.3.cloned.1.call-start = ((), (), s32[]{:S(2)}) async-start(), calls=%async_computation.1 | async-start | bytes 3145728 | tf_op jit(solution)/shard_map/psum | solution.py:64
  64.3 3.4 copy-start.2
  69.0 7.1 %copy-start = (f32[2048,512]{1,0:T(8,128)}, f32[2048,512]{1,0:T(8,128)S(1)}, u32[]{:S(2)}) copy-start(f32[2048,512]{1,0:T(8,128)S(1)} %multiply_multiply_fusion.1) | copy-start | bytes 12582916
  69.0 35.3 %copy-start.7 = (s32[2,768]{1,0:T(2,128)S(1)}, s32[2,768]{1,0:T(2,128)}, u32[]{:S(2)}) copy-start(s32[2,768]{1,0:T(2,128)} %param.7) | copy-start | bytes 18436
  76.1 25.4 %collective-permute-start = (f32[512,512]{0,1:T(8,128)S(1)}, f32[512,512]{0,1:T(8,128)S(1)}, u32[]{:S(2)}, u32[]{:S(2)}) collective-permute-start(f32[512,512]{0,1:T(8,128)S(1)} %fusion.54), channel_id=1, source_target_pairs={{0,32},{32,0},{64,96},{96,64},{128,160},{160,128},{192,224},{224,1... | collective-permute-start | bytes 3145736 | tf_op jit(solution)/shard_map/ppermute | solution.py:59
  101.7 48.0 %collective-permute-start.1 = (f32[512,512]{0,1:T(8,128)S(1)}, f32[512,512]{0,1:T(8,128)S(1)}, u32[]{:S(2)}, u32[]{:S(2)}) collective-permute-start(f32[512,512]{0,1:T(8,128)S(1)} %add.53), channel_id=1, source_target_pairs={{0,64},{32,96},{64,0},{96,32},{128,192},{160,224},{192,128},{224,1... | collective-permute-start | bytes 3145736 | tf_op jit(solution)/shard_map/ppermute | solution.py:59
  149.9 52.2 %collective-permute-start.2 = (f32[512,512]{0,1:T(8,128)S(1)}, f32[512,512]{0,1:T(8,128)S(1)}, u32[]{:S(2)}, u32[]{:S(2)}) collective-permute-start(f32[512,512]{0,1:T(8,128)S(1)} %add.54), channel_id=1, source_target_pairs={{0,128},{32,160},{64,192},{96,224},{128,0},{160,32},{192,64},{224,... | collective-permute-start | bytes 3145736 | tf_op jit(solution)/shard_map/ppermute | solution.py:59
  155.9 2.4 copy-start.3
  296.8 46.7 %copy-start.6 = (f32[512,512]{1,0:T(8,128)}, f32[512,512]{1,0:T(8,128)S(1)}, u32[]{:S(2)}) copy-start(f32[512,512]{1,0:T(8,128)S(1)} %get-tuple-element.91) | copy-start | bytes 3145732
  337.0 6.6 %copy-start.1 = (f32[2048,512]{1,0:T(8,128)S(1)}, f32[2048,512]{1,0:T(8,128)}, u32[]{:S(2)}) copy-start(f32[2048,512]{1,0:T(8,128)} %copy-done) | copy-start | bytes 12582916
  343.6 13.4 %slice-start = ((s8[6291456]{0:T(1024)(128)(4,1)}), s8[4194304]{0:T(1024)(128)(4,1)S(1)}, s32[]{:S(2)}) async-start(s8[6291456]{0:T(1024)(128)(4,1)} %bitcast.62), calls=%async_computation.2 | async-start | bytes 8388608
  348.2 8.7 %slice-start.1 = ((s8[6291456]{0:T(1024)(128)(4,1)}), s8[2097152]{0:T(1024)(128)(4,1)S(1)}, s32[]{:S(2)}) async-start(s8[6291456]{0:T(1024)(128)(4,1)} %bitcast.62), calls=%async_computation.3 | async-start | bytes 4194304
  355.9 1.0 copy-start.5
  444.3 23.9 %copy-start.4 = (f32[512,768]{1,0:T(8,128)S(1)}, f32[512,768]{1,0:T(8,128)}, u32[]{:S(2)}) copy-start(f32[512,768]{1,0:T(8,128)} %all-reduce.3.cloned.1.call-done) | copy-start | bytes 4718596
Sparse Core Ops, SparseCore 0:
  11.1 53.1 all-gather.3
  368.6 75.5 all-reduce.2
